TPU v7x, 32 devices: a whole 2x2x4 slice. The times are simulated.
32 devices in a mesh: dp: 4 (over y, x), tensor: 8 (over z, core).
Axes of the slice: x: 2, y: 2, z: 4, core: 2. Of those that a mesh axis runs over, the one named last changes fastest.
Arguments:
- inputs: bfloat16 [8192, 1024], P(('dp', 'tensor')), may hold values from -6 to 6
- project: bfloat16 [3, 1024, 1024], P(None, None, 'tensor'), may hold values from -0.25 to 0.25
- offsets: float32 [2, 1024], P(None, 'tensor'), may hold values from -3 to 3
- combine: bfloat16 [1024, 1024], P('tensor'), may hold values from -0.75 to 0.75
- combine_bias: float32 [1024], replicated, may hold values from -2 to 2
- norm_gain: float32 [2, 1024], replicated, may hold values from 0.25 to 1.75
- norm_shift: float32 [2, 1024], replicated, may hold values from -2 to 2
- expand: bfloat16 [1024, 4096], P(None, 'tensor'), may hold values from -0.1875 to 0.1875
- expand_bias: float32 [4096], P('tensor'), may hold values from -3 to 3
- contract: bfloat16 [4096, 1024], P('tensor'), may hold values from -0.09375 to 0.09375
- contract_bias: float32 [1024], replicated, may hold values from -2 to 2
- cotangent: bfloat16 [8192, 1024], P(('dp', 'tensor')), may hold values from -16 to 16
Outputs:
- block_out: bfloat16 [8192, 1024], P(('dp', 'tensor'))
- input_grad: bfloat16 [8192, 1024], P(('dp', 'tensor'))
- project_grad: float32 [3, 1024, 1024], P(None, None, 'tensor')
- offset_grad: float32 [2, 1024], P(None, 'tensor')
- combine_grad: float32 [1024, 1024], P('tensor')
- mixing_grad: float32 [1024], replicated
- gain_grad: float32 [2, 1024], replicated
- shift_grad: float32 [2, 1024], replicated
- expand_grad: float32 [1024, 4096], P(None, 'tensor')
- widening_grad: float32 [4096], P('tensor')
- contract_grad: float32 [4096, 1024], P('tensor')
- narrowing_grad: float32 [1024], replicated
All inputs are finite; a program needn't handle non-finite values.
Results may differ from a plain program's by a relative error of at most 0.02.
Values may be sent and summed in bfloat16 or wider, within the bound.
No kernel may reach another device: no remote copies, remote signals or barrier semaphores. Data moves between devices by JAX's collectives and lax.ppermute only.
A program may use at most 128 MiB of HBM per device.

v0:
```python
import math
import jax
import jax.numpy as jnp
from jax import lax
from jax.sharding import PartitionSpec as P

L = 2048
QBLOCK = 512
SEQ_DEV = 1
HEAD_DIM = 64


def layer_norm(features, gain_row, shift_row):
    center = features - jnp.mean(features, axis=-1, keepdims=True)
    spread = jnp.mean(center * center, axis=-1, keepdims=True)
    return center * lax.rsqrt(spread + 1e-06) * gain_row + shift_row


def gelu_exact(values):
    return jax.nn.gelu(values, approximate=False)


def attend_forward(queries, keys_all, values_all):
    scale_factor = 1.0 / math.sqrt(HEAD_DIM)

    def one_sequence(sequence_items):
        query_seq, key_seq, value_seq = sequence_items
        heads_here = query_seq.shape[1]

        def one_block(query_blk):
            scores = (
                jnp.einsum("qhe,khe->hqk", query_blk, key_seq, preferred_element_type=jnp.float32)
                * scale_factor
            )
            highest = jnp.max(scores, axis=-1, keepdims=True)
            raised = jnp.exp(scores - highest)
            summed = jnp.sum(raised, axis=-1, keepdims=True)
            weights = (raised / summed).astype(jnp.bfloat16)
            result = jnp.einsum(
                "hqk,khe->qhe", weights, value_seq, preferred_element_type=jnp.float32
            )
            return (result.astype(jnp.bfloat16), (highest + jnp.log(summed))[:, :, 0])

        blocks = query_seq.reshape(L // QBLOCK, QBLOCK, heads_here, HEAD_DIM)
        results, log_totals = lax.map(one_block, blocks)
        return (results.reshape(L, heads_here, HEAD_DIM), log_totals)

    return lax.map(one_sequence, (queries, keys_all, values_all))


def attend_backward(queries, keys_all, values_all, grad_out, log_totals):
    scale_factor = 1.0 / math.sqrt(HEAD_DIM)

    def one_sequence(sequence_items):
        query_seq, key_seq, value_seq, grad_seq, total_seq = sequence_items
        heads_here = query_seq.shape[1]
        shape_blocks = (L // QBLOCK, QBLOCK, heads_here, HEAD_DIM)

        def one_block(carried, block_items):
            key_grad, value_grad = carried
            query_blk, grad_blk, total_blk = block_items
            scores = (
                jnp.einsum("qhe,khe->hqk", query_blk, key_seq, preferred_element_type=jnp.float32)
                * scale_factor
            )
            probs = jnp.exp(scores - total_blk[:, :, None])
            grad_probs = jnp.einsum(
                "qhe,khe->hqk", grad_blk, value_seq, preferred_element_type=jnp.float32
            )
            row_dots = jnp.sum(probs * grad_probs, axis=-1, keepdims=True)
            grad_scores = (probs * (grad_probs - row_dots)).astype(jnp.bfloat16)
            query_grad = (
                jnp.einsum("hqk,khe->qhe", grad_scores, key_seq, preferred_element_type=jnp.float32)
                * scale_factor
            )
            key_grad = (
                key_grad
                + jnp.einsum(
                    "hqk,qhe->khe", grad_scores, query_blk, preferred_element_type=jnp.float32
                )
                * scale_factor
            )
            value_grad = value_grad + jnp.einsum(
                "hqk,qhe->khe",
                probs.astype(jnp.bfloat16),
                grad_blk,
                preferred_element_type=jnp.float32,
            )
            return ((key_grad, value_grad), query_grad)

        empty = jnp.zeros((L, heads_here, HEAD_DIM), jnp.float32)
        (key_grad, value_grad), query_grad = lax.scan(
            one_block,
            (empty, empty),
            (query_seq.reshape(shape_blocks), grad_seq.reshape(shape_blocks), total_seq),
        )
        return (query_grad.reshape(L, heads_here, HEAD_DIM), key_grad, value_grad)

    return lax.map(one_sequence, (queries, keys_all, values_all, grad_out, log_totals))


def per_device(
    inputs,
    project,
    offsets,
    combine,
    combine_bias,
    norm_gain,
    norm_shift,
    expand,
    expand_bias,
    contract,
    contract_bias,
    cotangent,
):
    local_cols = project.shape[2]
    heads_here = local_cols // HEAD_DIM
    group_rows = SEQ_DEV * L
    row_values = inputs.astype(jnp.float32)
    normed_one, back_one = jax.vjp(layer_norm, row_values, norm_gain[0], norm_shift[0])
    normed_full = lax.all_gather(normed_one.astype(jnp.bfloat16), "tensor", axis=0, tiled=True)
    mapped = jnp.einsum("td,kde->tke", normed_full, project, preferred_element_type=jnp.float32)
    bias_rows = jnp.stack([offsets[0], jnp.zeros_like(offsets[0]), offsets[1]])
    mapped = (mapped + bias_rows[None]).astype(jnp.bfloat16)
    head_split = mapped.reshape(SEQ_DEV, L, 3, heads_here, HEAD_DIM)
    queries = head_split[:, :, 0]
    keys_all = head_split[:, :, 1]
    values_all = head_split[:, :, 2]
    attended, log_totals = attend_forward(queries, keys_all, values_all)
    attended = attended.reshape(group_rows, local_cols)
    block_rows = attended
    branch = lax.psum_scatter(
        jnp.dot(block_rows, combine, preferred_element_type=jnp.float32).astype(jnp.bfloat16),
        "tensor",
        scatter_dimension=0,
        tiled=True,
    ).astype(jnp.float32)
    hidden = row_values + (branch + combine_bias)
    normed_two, back_two = jax.vjp(layer_norm, hidden, norm_gain[1], norm_shift[1])
    hidden_full = lax.all_gather(normed_two.astype(jnp.bfloat16), "tensor", axis=0, tiled=True)
    before = jnp.dot(hidden_full, expand, preferred_element_type=jnp.float32) + expand_bias
    active, gelu_back = jax.vjp(gelu_exact, before)
    active_low = active.astype(jnp.bfloat16)
    block_rows = active_low
    mixed = lax.psum_scatter(
        jnp.dot(block_rows, contract, preferred_element_type=jnp.float32).astype(jnp.bfloat16),
        "tensor",
        scatter_dimension=0,
        tiled=True,
    ).astype(jnp.float32)
    block_out = (hidden + mixed + contract_bias).astype(jnp.bfloat16)
    grad_local = cotangent.astype(jnp.float32)
    grad_full = lax.all_gather(cotangent, "tensor", axis=0, tiled=True)
    contract_grad = jnp.einsum(
        "tf,td->fd", active_low, grad_full, preferred_element_type=jnp.float32
    )
    grad_active = jnp.einsum("td,fd->tf", grad_full, contract, preferred_element_type=jnp.float32)
    grad_before = gelu_back(grad_active)[0].astype(jnp.bfloat16)
    widening_grad = jnp.sum(grad_before.astype(jnp.float32), axis=0)
    expand_grad = jnp.einsum(
        "td,tf->df", hidden_full, grad_before, preferred_element_type=jnp.float32
    )
    block_rows = grad_before
    grad_normed_two = lax.psum_scatter(
        jnp.einsum("tf,df->td", block_rows, expand, preferred_element_type=jnp.float32).astype(
            jnp.bfloat16
        ),
        "tensor",
        scatter_dimension=0,
        tiled=True,
    ).astype(jnp.float32)
    grad_hidden_norm, gain_two_grad, shift_two_grad = back_two(grad_normed_two)
    grad_hidden = grad_local + grad_hidden_norm
    grad_branch = grad_hidden.astype(jnp.bfloat16)
    branch_full = lax.all_gather(grad_branch, "tensor", axis=0, tiled=True)
    combine_grad = jnp.einsum(
        "te,td->ed", attended, branch_full, preferred_element_type=jnp.float32
    )
    grad_attended = jnp.einsum(
        "td,ed->te", branch_full, combine, preferred_element_type=jnp.float32
    ).astype(jnp.bfloat16)
    query_grad, key_grad, value_grad = attend_backward(
        queries,
        keys_all,
        values_all,
        grad_attended.reshape(SEQ_DEV, L, heads_here, HEAD_DIM),
        log_totals,
    )
    grad_mapped = (
        jnp.stack([query_grad, key_grad, value_grad], axis=2)
        .reshape(group_rows, 3, local_cols)
        .astype(jnp.bfloat16)
    )
    mapped_sums = jnp.sum(grad_mapped.astype(jnp.float32), axis=0)
    offset_grad = jnp.stack([mapped_sums[0], mapped_sums[2]])
    project_grad = jnp.einsum(
        "td,tke->kde", normed_full, grad_mapped, preferred_element_type=jnp.float32
    )
    block_rows = grad_mapped
    grad_normed_one = lax.psum_scatter(
        jnp.einsum("tke,kde->td", block_rows, project, preferred_element_type=jnp.float32).astype(
            jnp.bfloat16
        ),
        "tensor",
        scatter_dimension=0,
        tiled=True,
    ).astype(jnp.float32)
    grad_input_norm, gain_one_grad, shift_one_grad = back_one(grad_normed_one)
    input_grad = (grad_hidden + grad_input_norm).astype(jnp.bfloat16)
    project_grad, offset_grad, combine_grad, expand_grad, widening_grad, contract_grad = (
        lax.psum(project_grad.astype(jnp.bfloat16), "dp").astype(jnp.float32),
        lax.psum(offset_grad.astype(jnp.bfloat16), "dp").astype(jnp.float32),
        lax.psum(combine_grad.astype(jnp.bfloat16), "dp").astype(jnp.float32),
        lax.psum(expand_grad.astype(jnp.bfloat16), "dp").astype(jnp.float32),
        lax.psum(widening_grad.astype(jnp.bfloat16), "dp").astype(jnp.float32),
        lax.psum(contract_grad.astype(jnp.bfloat16), "dp").astype(jnp.float32),
    )
    mixing_part = jnp.sum(grad_branch.astype(jnp.float32), axis=0)
    narrowing_part = jnp.sum(grad_local, axis=0)
    gain_part = jnp.stack([gain_one_grad, gain_two_grad])
    shift_part = jnp.stack([shift_one_grad, shift_two_grad])
    mixing_grad, gain_grad, shift_grad, narrowing_grad = lax.psum(
        (mixing_part, gain_part, shift_part, narrowing_part), ("dp", "tensor")
    )
    return (
        block_out,
        input_grad,
        project_grad,
        offset_grad,
        combine_grad,
        mixing_grad,
        gain_grad,
        shift_grad,
        expand_grad,
        widening_grad,
        contract_grad,
        narrowing_grad,
    )


def solution(mesh):
    placed = (
        P(("dp", "tensor"), None),
        P(None, None, "tensor"),
        P(None, "tensor"),
        P("tensor", None),
        P(),
        P(),
        P(),
        P(None, "tensor"),
        P("tensor"),
        P("tensor", None),
        P(),
        P(("dp", "tensor"), None),
    )
    return jax.shard_map(
        per_device,
        mesh=mesh,
        in_specs=placed,
        out_specs=(
            P(("dp", "tensor"), None),
            P(("dp", "tensor"), None),
            P(None, None, "tensor"),
            P(None, "tensor"),
            P("tensor", None),
            P(),
            P(),
            P(),
            P(None, "tensor"),
            P("tensor"),
            P("tensor", None),
            P(),
        ),
        check_vma=False,
    )
```

profile of v0, /device:TPU:12, one launch (start us, length us, event | category | flops | bytes accessed | tf_op | source)
XLA Modules:
  0.0 682.0 jit_solution(15915693320500464593)
XLA Ops:
  12.0 2.1 fusion.63
  15.8 45.2 %all-gather.5.cloned.1.call-done = bf16[2048,1024]{1,0:T(8,128)(2,1)} async-done(((bf16[256,1024]{1,0:T(8,128)(2,1)}), bf16[2048,1024]{1,0:T(8,128)(2,1)}) %all-gather.5.cloned.1.call-update) | async-done | bytes 4194320 | tf_op jit(solution)/shard_map/all_gather | solution.py:121
  61.0 4.0 fusion.84
  65.9 23.8 %while.47 = (s32[]{:T(128)}, bf16[4,512,2,64]{1,3,2,0:T(8,128)(2,1)}, f32[4,2,512]{2,1,0:T(2,128)S(1)}, bf16[4,512,2,64]{1,3,2,0:T(8,128)(2,1)S(1)}, bf16[2048,2...) while((s32[]{:T(128)}, bf16[4,512,2,64]{1,3,2,0:T(8,128)(2,1)}, ...), condition=%wide.region_5.0_spmd, body=%wide.region_2.5_spmd.sunk | while | flops 555809792 | bytes 26509408 | solution.py:45
  69.0 2.9 fusion.134
  74.9 2.9 fusion.134
  80.9 2.9 fusion.134
  86.8 2.9 fusion.134
  89.7 1.8 copy.33
  92.5 3.3 convolution_convert_fusion.2
  95.9 47.0 %reduce-scatter.5.cloned.1.call-done = bf16[256,1024]{1,0:T(8,128)(2,1)} async-done(((bf16[2048,1024]{1,0:T(8,128)(2,1)}), bf16[256,1024]{1,0:T(8,128)(2,1)}) %reduce-scatter.5.cloned.1.call-update) | async-done | bytes 524304 | tf_op jit(solution)/shard_map/reduce_scatter | solution.py:132
  145.5 2.1 add_convert_fusion.4
  148.5 46.5 %all-gather.7.cloned.1.call-done = bf16[2048,1024]{1,0:T(8,128)(2,1)} async-done(((bf16[256,1024]{1,0:T(8,128)(2,1)}), bf16[2048,1024]{1,0:T(8,128)(2,1)}) %all-gather.7.cloned.1.call-update) | async-done | bytes 4194320 | tf_op jit(solution)/shard_map/all_gather | solution.py:140
  195.0 6.8 fusion.85
  201.8 40.4 %all-gather.9.cloned.1.call-done = bf16[2048,1024]{1,0:T(8,128)(2,1)} async-done(((bf16[256,1024]{1,0:T(8,128)(2,1)}), bf16[2048,1024]{1,0:T(8,128)(2,1)}) %all-gather.9.cloned.1.call-update) | async-done | bytes 4194320 | tf_op jit(solution)/shard_map/all_gather | solution.py:153
  242.2 15.1 %fusion.77 = (bf16[512]{0:T(512)(128)(2,1)S(1)}, bf16[2048,512]{1,0:T(8,128)(2,1)S(1)}, f32[2048,512]{1,0:T(8,128)}) fusion(f32[2048,512]{1,0:T(8,128)} %fusion.85, f32[512]{0:T(512)S(1)} %copy-done.31, bf16[2048,1024]{1,0:T(8,128)(2,1)} %all-gather.9.cloned.1.call-done, bf16[512,1024]{1,0:T(8,128)(2,1)S(1)} %copy-done), kind=kOutput, calls=%fused_computation.130 | convolution fusion | flops 2225077760 | bytes 15731712 | tf_op jit(solution)/shard_map/td,fd->tf/dot_general | solution.py:157
  258.6 4.3 convolution_convert_fusion
  263.0 4.6 multiply_convert_fusion.1
  268.9 4.3 convolution_convert_fusion.1
  273.5 36.5 %reduce-scatter.9.cloned.1.call-done = bf16[256,1024]{1,0:T(8,128)(2,1)} async-done(((bf16[2048,1024]{1,0:T(8,128)(2,1)}), bf16[256,1024]{1,0:T(8,128)(2,1)}) %reduce-scatter.9.cloned.1.call-update) | async-done | bytes 524304 | tf_op jit(solution)/shard_map/reduce_scatter | solution.py:164
  311.5 49.0 %reduce-scatter.7.cloned.1.call-done = bf16[256,1024]{1,0:T(8,128)(2,1)} async-done(((bf16[2048,1024]{1,0:T(8,128)(2,1)}), bf16[256,1024]{1,0:T(8,128)(2,1)}) %reduce-scatter.7.cloned.1.call-update) | async-done | bytes 524304 | tf_op jit(solution)/shard_map/reduce_scatter | solution.py:145
  360.5 2.5 fusion.79
  365.2 6.4 convolution_convert_fusion.5
  371.6 3.3 convolution_convert_fusion.4
  374.9 37.5 %all-gather.11.cloned.1.call-done = bf16[2048,1024]{1,0:T(8,128)(2,1)} async-done(((bf16[256,1024]{1,0:T(8,128)(2,1)}), bf16[2048,1024]{1,0:T(8,128)(2,1)}) %all-gather.11.cloned.1.call-update) | async-done | bytes 4194320 | tf_op jit(solution)/shard_map/all_gather | solution.py:175
  412.4 4.2 convolution_convert_fusion.3
  416.7 3.2 reshape.179
  419.8 3.5 copy.36
  423.4 49.0 %while.48 = (s32[]{:T(128)}, f32[2048,2,64]{0,2,1:T(8,128)S(1)}, f32[2048,2,64]{0,2,1:T(8,128)S(1)}, bf16[4,512,2,64]{1,3,2,0:T(8,128)(2,1)}, bf16[4,512,2,64]{1...) while((s32[]{:T(128)}, f32[2048,2,64]{0,2,1:T(8,128)S(1)}, ...), condition=%wide.region_15.16_spmd.clone, body=%wide.region_13.15_spmd.clone.sunk | while | flops 1368718336 | bytes 77885704 | solution.py:92
  423.4 2.2 fusion.144
  425.6 1.9 fusion.146
  427.6 2.4 multiply_reduce_fusion.6
  430.0 2.1 multiply_convert_fusion.3
  433.5 2.0 fusion.145
  435.6 2.3 fusion.144
  437.9 1.9 fusion.146
  439.8 2.4 multiply_reduce_fusion.6
  442.3 2.1 multiply_convert_fusion.3
  445.8 2.0 fusion.145
  447.9 2.3 fusion.144
  450.1 1.9 fusion.146
  452.1 2.4 multiply_reduce_fusion.6
  454.5 2.1 multiply_convert_fusion.3
  458.0 2.0 fusion.145
  460.1 2.3 fusion.144
  462.4 1.9 fusion.146
  464.3 2.4 multiply_reduce_fusion.6
  466.8 2.1 multiply_convert_fusion.3
  470.3 2.0 fusion.145
  472.3 3.6 copy.46
  476.0 3.1 reshape.180
  479.9 2.1 copy.39
  482.4 3.8 convolution_convert_fusion.6
  486.2 2.7 fusion.55
  489.2 5.5 bitcast_convert_fusion
  495.0 9.5 %all-reduce.1 = (bf16[2,128]{1,0:T(2,128)(2,1)S(1)}, bf16[512]{0:T(512)(128)(2,1)S(1)}) all-reduce(bf16[2,128]{1,0:T(2,128)(2,1)S(1)} %pad_maximum_fusion.4, bf16[512]{0:T(512)(128)(2,1)S(1)} %get-tuple-element.271), channel_id=1, replica_groups=mesh['dp'=4,'tensor'=8] {'dp'}, use_global_device_ids=true, to_apply=%region_21.22 | all-reduce | flops 768 | bytes 3072 | tf_op jit(solution)/shard_map/psum | solution.py:212
  505.6 70.6 %all-reduce.5.cloned.1.call-done = (bf16[3,1024,128]{1,2,0:T(8,128)(2,1)}, bf16[128,1024]{1,0:T(8,128)(2,1)}, bf16[1024,512]{1,0:T(8,128)(2,1)}, bf16[512,1024]{1,0:T(8,128)(2,1)}) async-done(((bf16[3,1024,128]{1,2,0:T(8,128)(2,1)}, bf16[128,1024]{1,0:T(8,128)(2,1)}, bf16[1024,512]{1,0:T(8,128)(2,1)}, bf16[512,1024]{1,0:T(8,128)(2,1)}), (bf16[3,1024,128]{1,2,0:T(8,128)(2,1)}, bf16[128,1024]{1,0:T(8,128)(2,1)}, ...) | async-done | bytes 3145744 | tf_op jit(solution)/shard_map/psum | solution.py:211
  576.2 1.8 convert_element_type.140
  578.0 2.6 copy.42
  580.6 3.0 convert_element_type.143
  583.6 2.9 convert_element_type.146
  586.4 39.1 %reduce-scatter.11.cloned.1.call-done = bf16[256,1024]{1,0:T(8,128)(2,1)} async-done(((bf16[2048,1024]{1,0:T(8,128)(2,1)}), bf16[256,1024]{1,0:T(8,128)(2,1)}) %reduce-scatter.11.cloned.1.call-update) | async-done | bytes 524304 | tf_op jit(solution)/shard_map/reduce_scatter | solution.py:200
  628.7 2.4 convert_reduce_fusion.3
  631.1 43.9 %all-reduce = (f32[1024]{0:T(1024)}, f32[2,1024]{1,0:T(2,128)}, f32[2,1024]{1,0:T(2,128)}, f32[1024]{0:T(1024)}) all-reduce(f32[1024]{0:T(1024)S(1)} %get-tuple-element.269, f32[2,1024]{1,0:T(2,128)S(1)} %get-tuple-element.294, f32[2,1024]{1,0:T(2,128)S(1)} %get-tuple-element.295, ...), channel_id=1, replica_groups=mesh['dp'=4,'tensor'=8] {'dp','tensor'}, use_global_device_ids=true, to_apply=%region_24.25 | all-reduce | flops 6144 | bytes 49152 | tf_op jit(solution)/shard_map/psum | solution.py:222
  (177 shorter events, 42.3 us)
Async XLA Ops:
  7.2 235.0 %copy-start = (bf16[512,1024]{1,0:T(8,128)(2,1)S(1)}, bf16[512,1024]{1,0:T(8,128)(2,1)}, u32[]{:S(2)}) copy-start(bf16[512,1024]{1,0:T(8,128)(2,1)} %param.25) | copy-start | bytes 3145732
  7.2 8.5 %copy-start.32 = (f32[2,128]{1,0:T(2,128)S(1)}, f32[2,128]{1,0:T(2,128)}, u32[]{:S(2)}) copy-start(f32[2,128]{1,0:T(2,128)} %param.18) | copy-start | bytes 3076
  7.2 53.8 %all-gather.5.cloned.1.call-start = ((), (), s32[]{:S(2)}) async-start(), calls=%async_computation.4 | async-start | bytes 4718592 | tf_op jit(solution)/shard_map/all_gather | solution.py:121
  8.5 5.7 copy-start.24
  9.9 0.6 copy-start.28
  10.4 3.7 copy-start.26
  11.2 3.0 copy-start.22
  14.2 128.7 %reduce-scatter.5.cloned.1.call-start = ((), (), s32[]{:S(2)}) async-start(), calls=%async_computation.5 | async-start | bytes 4718592 | tf_op jit(solution)/shard_map/reduce_scatter | solution.py:132
  65.9 26.6 %copy-start.20 = (bf16[128,1024]{1,0:T(8,128)(2,1)S(1)}, bf16[128,1024]{1,0:T(8,128)(2,1)}, u32[]{:S(2)}) copy-start(bf16[128,1024]{1,0:T(8,128)(2,1)} %param.19) | copy-start | bytes 786436
  89.7 2.0 copy-start.3
  89.7 6.1 copy-start.6
  91.7 0.8 copy-start.9
  95.8 47.0 %copy-start.2 = (bf16[256,1024]{1,0:T(8,128)(2,1)S(1)}, bf16[256,1024]{1,0:T(8,128)(2,1)}, u32[]{:S(2)}) copy-start(bf16[256,1024]{1,0:T(8,128)(2,1)} %param.16) | copy-start | bytes 1572868
  95.8 47.0 %copy-start.21 = (f32[1024]{0:T(1024)S(1)}, f32[1024]{0:T(1024)}, u32[]{:S(2)}) copy-start(f32[1024]{0:T(1024)} %param.20) | copy-start | bytes 12292
  95.8 99.2 %all-gather.7.cloned.1.call-start = ((), (), s32[]{:S(2)}) async-start(), calls=%async_computation.6 | async-start | bytes 4718592 | tf_op jit(solution)/shard_map/all_gather | solution.py:140
  147.7 94.5 %all-gather.9.cloned.1.call-start = ((), (), s32[]{:S(2)}) async-start(), calls=%async_computation.8 | async-start | bytes 4718592 | tf_op jit(solution)/shard_map/all_gather | solution.py:153
  148.2 93.9 %copy-start.31 = (f32[512]{0:T(512)S(1)}, f32[512]{0:T(512)}, u32[]{:S(2)}) copy-start(f32[512]{0:T(512)} %param.24) | copy-start | bytes 6148
  148.3 161.7 %reduce-scatter.9.cloned.1.call-start = ((), (), s32[]{:S(2)}) async-start(), calls=%async_computation.9 | async-start | bytes 4718592 | tf_op jit(solution)/shard_map/reduce_scatter | solution.py:164
  242.2 16.4 %copy-start.35 = (bf16[1024,512]{1,0:T(8,128)(2,1)S(1)}, bf16[1024,512]{1,0:T(8,128)(2,1)}, u32[]{:S(2)}) copy-start(bf16[1024,512]{1,0:T(8,128)(2,1)} %param.23) | copy-start | bytes 3145732
  257.3 1.3 copy-start.36
  262.9 97.6 %reduce-scatter.7.cloned.1.call-start = ((), (), s32[]{:S(2)}) async-start(), calls=%async_computation.7 | async-start | bytes 4718592 | tf_op jit(solution)/shard_map/reduce_scatter | solution.py:145
  267.6 1.3 copy-start.16
  273.2 36.8 %copy-start.5 = (bf16[256,1024]{1,0:T(8,128)(2,1)S(1)}, bf16[256,1024]{1,0:T(8,128)(2,1)}, u32[]{:S(2)}) copy-start(bf16[256,1024]{1,0:T(8,128)(2,1)} %reduce-scatter.5.cloned.1.call-done) | copy-start | bytes 1572868
  273.2 87.3 %copy-start.30 = (f32[1024]{0:T(1024)S(1)}, f32[1024]{0:T(1024)}, u32[]{:S(2)}) copy-start(f32[1024]{0:T(1024)} %param.26) | copy-start | bytes 12292
  273.2 90.9 %copy-start.12 = (bf16[256,1024]{1,0:T(8,128)(2,1)S(1)}, bf16[256,1024]{1,0:T(8,128)(2,1)}, u32[]{:S(2)}) copy-start(bf16[256,1024]{1,0:T(8,128)(2,1)} %param.27) | copy-start | bytes 1572868
  273.2 139.2 %all-gather.11.cloned.1.call-start = ((), (), s32[]{:S(2)}) async-start(), calls=%async_computation.10 | async-start | bytes 4718592 | tf_op jit(solution)/shard_map/all_gather | solution.py:175
  363.1 1.0 copy-start.7
  365.1 211.1 %all-reduce.5.cloned.1.call-start = ((), (), s32[]{:S(2)}) async-start(), calls=%async_computation.12 | async-start | bytes 6291456 | tf_op jit(solution)/shard_map/psum | solution.py:211
  365.2 6.4 copy-start.17
  365.2 6.4 copy-start.34
  423.4 2.2 copy-start.11
  425.6 1.9 copy-start.4
  430.0 2.1 copy-start.18
  433.5 2.0 copy-start.19
  435.6 2.3 copy-start.11
  437.9 1.9 copy-start.4
  442.3 2.1 copy-start.18
  445.8 2.1 copy-start.19
  447.8 2.3 copy-start.11
  450.1 1.9 copy-start.4
  454.5 2.1 copy-start.18
  458.0 2.1 copy-start.19
  460.1 2.3 copy-start.11
  462.4 1.9 copy-start.4
  466.8 2.1 copy-start.18
  470.3 2.1 copy-start.19
  472.3 10.0 %copy-start.10 = (bf16[16,8,4,512]{3,1,2,0:T(8,128)(2,1)S(1)}, bf16[16,8,4,512]{3,1,2,0:T(8,128)(2,1)}, u32[]{:S(2)}) copy-start(bf16[16,8,4,512]{3,1,2,0:T(8,128)(2,1)} %copy-done.9) | copy-start | bytes 1572868
  479.9 6.2 copy-start.14
  482.1 4.1 copy-start.15
  482.4 3.8 copy-start.33
  488.9 136.6 %reduce-scatter.11.cloned.1.call-start = ((), (), s32[]{:S(2)}) async-start(), calls=%async_computation.11 | async-start | bytes 4718592 | tf_op jit(solution)/shard_map/reduce_scatter | solution.py:200
  578.0 47.5 %copy-start.23 = (f32[1,1024]{1,0:T(1,128)S(1)}, f32[1,1024]{1,0:T(1,128)}, u32[]{:S(2)}) copy-start(f32[1,1024]{1,0:T(1,128)} %copy-done.22) | copy-start | bytes 12292
  578.0 47.5 %copy-start.25 = (f32[256]{0:T(256)S(1)}, f32[256]{0:T(256)}, u32[]{:S(2)}) copy-start(f32[256]{0:T(256)} %copy-done.24) | copy-start | bytes 3076
  580.6 46.4 %copy-start.29 = (f32[256]{0:T(256)S(1)}, f32[256]{0:T(256)}, u32[]{:S(2)}) copy-start(f32[256]{0:T(256)} %copy-done.28) | copy-start | bytes 3076
  580.6 46.4 %copy-start.27 = (f32[256]{0:T(256)S(1)}, f32[256]{0:T(256)}, u32[]{:S(2)}) copy-start(f32[256]{0:T(256)} %copy-done.26) | copy-start | bytes 3076
  580.6 48.1 %copy-start.8 = (f32[256,1024]{1,0:T(8,128)S(1)}, f32[256,1024]{1,0:T(8,128)}, u32[]{:S(2)}) copy-start(f32[256,1024]{1,0:T(8,128)} %copy-done.7) | copy-start | bytes 3145732
  580.6 48.1 %copy-start.13 = (bf16[256,1024]{1,0:T(8,128)(2,1)S(1)}, bf16[256,1024]{1,0:T(8,128)(2,1)}, u32[]{:S(2)}) copy-start(bf16[256,1024]{1,0:T(8,128)(2,1)} %param.27) | copy-start | bytes 1572868
  583.6 91.5 %copy-start.1 = (bf16[512,1024]{1,0:T(8,128)(2,1)S(1)}, bf16[512,1024]{1,0:T(8,128)(2,1)}, u32[]{:S(2)}) copy-start(bf16[512,1024]{1,0:T(8,128)(2,1)} %param.25) | copy-start | bytes 3145732
Sparse Core Ops, SparseCore 0:
  14.3 46.7 all-gather.4
  95.9 46.8 reduce-scatter.4
  147.8 47.1 all-gather.6
  196.5 45.6 all-gather.8
  263.1 46.8 reduce-scatter.8
  312.1 48.3 reduce-scatter.6
  365.2 47.1 all-gather.10
  489.0 87.1 all-reduce.4
  578.5 46.9 reduce-scatter.10
where the time goes:
time: 690 us; the launch traced here: 682 us
  waiting for transfers between devices  412 us (60%)
  matrix products  121 us (18%)
  blocking collectives  53.4 us (8%)
  other arithmetic  49.9 us (7%)
  local copies, waits for them, and re-layouts  29.1 us (4%)
  between operations  14.7 us (2%)
    psum x1, waiting for transfers between devices, per_device(): lax.psum(project_grad.astype(jnp.bfloat16), 'dp').astype(jnp.float32)  70.6 us
    reduce_scatter x1, waiting for transfers between devices, per_device(): lax.psum_scatter(jnp.dot(block_rows, contract, preferred_element_type=jnp...  49 us
    reduce_scatter x1, waiting for transfers between devices, per_device(): lax.psum_scatter(jnp.dot(block_rows, combine, preferred_element_type=jnp....  47 us
    all_gather x1, waiting for transfers between devices, per_device(): lax.all_gather(normed_two.astype(jnp.bfloat16), 'tensor', axis=0, tiled=T...  46.5 us
    all_gather x1, waiting for transfers between devices, per_device(): lax.all_gather(normed_one.astype(jnp.bfloat16), 'tensor', axis=0, tiled=T...  45.2 us
    psum x1, blocking collectives, per_device(): lax.psum((mixing_part, gain_part, shift_part, narrowing_part), ('dp', 'te...  43.9 us
    all_gather x1, waiting for transfers between devices, per_device(): grad_full = lax.all_gather(cotangent, 'tensor', axis=0, tiled=True)  40.4 us
    reduce_scatter x1, waiting for transfers between devices, per_device(): lax.psum_scatter(jnp.einsum('tke,kde->td', block_rows, project, preferred...  39.1 us
  transfers between devices with their start and end apart: 9, of which 9 were waited for; matrix products, arithmetic and copies ran while one was open for 7% of the time, Pallas kernels for 0%

commit v1 on v0

--- a/solution.py
+++ b/solution.py
@@ -3,6 +3,7 @@
 import jax.numpy as jnp
 from jax import lax
 from jax.sharding import PartitionSpec as P
+from jax.lax import all_gather
 
 L = 2048
 QBLOCK = 512
@@ -208,7 +209,7 @@
     grad_input_norm, gain_one_grad, shift_one_grad = back_one(grad_normed_one)
     input_grad = (grad_hidden + grad_input_norm).astype(jnp.bfloat16)
     project_grad, offset_grad, combine_grad, expand_grad, widening_grad, contract_grad = (
-        lax.psum(project_grad.astype(jnp.bfloat16), "dp").astype(jnp.float32),
+        jnp.sum(all_gather(project_grad.astype(jnp.bfloat16), "dp"), axis=0).astype(jnp.float32),
         lax.psum(offset_grad.astype(jnp.bfloat16), "dp").astype(jnp.float32),
         lax.psum(combine_grad.astype(jnp.bfloat16), "dp").astype(jnp.float32),
         lax.psum(expand_grad.astype(jnp.bfloat16), "dp").astype(jnp.float32),

time: 690 us -> 661 us (0.958)
  waiting for transfers between devices: 412 us -> 377 us
    psum x1, waiting for transfers between devices: 70.6 us -> 0.01 us  [per_device(): lax.psum(combine_grad.astype(jnp.bfloat16), 'dp').astype(jnp.float32)]
    all_gather x0 -> x1, waiting for transfers between devices: none -> 34 us  [per_device(): all_gather(project_grad.astype(jnp.bfloat16), 'dp')]
    unnamed x70 -> x69, local copies, waits for them, and re-layouts: 12.7 us -> 15.1 us
  transfers between devices with their start and end apart: 9 -> 10, of which waited for: 9 -> 9; matrix products, arithmetic and copies ran while one was open for 7% -> 17% of each run, Pallas kernels for 0% -> 0%
where the time goes in v1:
time: 661 us; the launch traced here: 653 us
  waiting for transfers between devices  377 us (57%)
  matrix products  123 us (19%)
  blocking collectives  53.2 us (8%)
  other arithmetic  51.3 us (8%)
  local copies, waits for them, and re-layouts  31.9 us (5%)
  between operations  15.1 us (2%)
    reduce_scatter x1, waiting for transfers between devices, per_device(): lax.psum_scatter(jnp.dot(block_rows, contract, preferred_element_type=jnp...  49 us
    reduce_scatter x1, waiting for transfers between devices, per_device(): lax.psum_scatter(jnp.dot(block_rows, combine, preferred_element_type=jnp....  47 us
    all_gather x1, waiting for transfers between devices, per_device(): lax.all_gather(normed_two.astype(jnp.bfloat16), 'tensor', axis=0, tiled=T...  46.5 us
    all_gather x1, waiting for transfers between devices, per_device(): lax.all_gather(normed_one.astype(jnp.bfloat16), 'tensor', axis=0, tiled=T...  45.2 us
    psum x1, blocking collectives, per_device(): lax.psum((mixing_part, gain_part, shift_part, narrowing_part), ('dp', 'te...  43.9 us
    reduce_scatter x1, waiting for transfers between devices, per_device(): lax.psum_scatter(jnp.einsum('tke,kde->td', block_rows, project, preferred...  40.5 us
    all_gather x1, waiting for transfers between devices, per_device(): grad_full = lax.all_gather(cotangent, 'tensor', axis=0, tiled=True)  40.4 us
    all_gather x1, waiting for transfers between devices, per_device(): branch_full = lax.all_gather(grad_branch, 'tensor', axis=0, tiled=True)  37.5 us
  transfers between devices with their start and end apart: 10, of which 9 were waited for; matrix products, arithmetic and copies ran while one was open for 17% of the time, Pallas kernels for 0%

profile of v1, /device:TPU:12, one launch (start us, length us, event | category | flops | bytes accessed | tf_op | source)
XLA Modules:
  0.0 652.9 jit_solution(15087079676683600755)
XLA Ops:
  12.0 2.1 fusion.63
  15.8 45.2 %all-gather.7.cloned.1.call-done = bf16[2048,1024]{1,0:T(8,128)(2,1)} async-done(((bf16[256,1024]{1,0:T(8,128)(2,1)}), bf16[2048,1024]{1,0:T(8,128)(2,1)}) %all-gather.7.cloned.1.call-update) | async-done | bytes 4194320 | tf_op jit(solution)/shard_map/all_gather | solution.py:122
  61.0 4.0 fusion.84
  65.9 23.8 %while.47 = (s32[]{:T(128)}, bf16[4,512,2,64]{1,3,2,0:T(8,128)(2,1)}, f32[4,2,512]{2,1,0:T(2,128)S(1)}, bf16[4,512,2,64]{1,3,2,0:T(8,128)(2,1)S(1)}, bf16[2048,2...) while((s32[]{:T(128)}, bf16[4,512,2,64]{1,3,2,0:T(8,128)(2,1)}, ...), condition=%wide.region_5.0_spmd, body=%wide.region_2.5_spmd.sunk | while | flops 555809792 | bytes 26509408 | solution.py:46
  69.0 2.9 fusion.134
  74.9 2.9 fusion.134
  80.9 2.9 fusion.134
  86.8 2.9 fusion.134
  92.5 3.3 convolution_convert_fusion.2
  95.9 47.0 %reduce-scatter.5.cloned.1.call-done = bf16[256,1024]{1,0:T(8,128)(2,1)} async-done(((bf16[2048,1024]{1,0:T(8,128)(2,1)}), bf16[256,1024]{1,0:T(8,128)(2,1)}) %reduce-scatter.5.cloned.1.call-update) | async-done | bytes 524304 | tf_op jit(solution)/shard_map/reduce_scatter | solution.py:133
  145.5 2.1 add_convert_fusion.4
  148.5 46.5 %all-gather.9.cloned.1.call-done = bf16[2048,1024]{1,0:T(8,128)(2,1)} async-done(((bf16[256,1024]{1,0:T(8,128)(2,1)}), bf16[2048,1024]{1,0:T(8,128)(2,1)}) %all-gather.9.cloned.1.call-update) | async-done | bytes 4194320 | tf_op jit(solution)/shard_map/all_gather | solution.py:141
  195.0 6.8 %fusion.85 = f32[2048,512]{1,0:T(8,128)} fusion(bf16[2048,1024]{1,0:T(8,128)(2,1)} %all-gather.9.cloned.1.call-done, bf16[1024,512]{1,0:T(8,128)(2,1)} %param.23), kind=kOutput, calls=%fused_computation.137 | convolution fusion | flops 2147483648 | bytes 9437184 | tf_op jit(solution)/shard_map/dot_general | solution.py:142
  201.8 40.4 %all-gather.11.cloned.1.call-done = bf16[2048,1024]{1,0:T(8,128)(2,1)} async-done(((bf16[256,1024]{1,0:T(8,128)(2,1)}), bf16[2048,1024]{1,0:T(8,128)(2,1)}) %all-gather.11.cloned.1.call-update) | async-done | bytes 4194320 | tf_op jit(solution)/shard_map/all_gather | solution.py:154
  242.2 15.1 %fusion.77 = (bf16[512]{0:T(512)(128)(2,1)S(1)}, bf16[2048,512]{1,0:T(8,128)(2,1)S(1)}, f32[2048,512]{1,0:T(8,128)}) fusion(f32[2048,512]{1,0:T(8,128)} %fusion.85, f32[512]{0:T(512)S(1)} %copy-done.31, bf16[2048,1024]{1,0:T(8,128)(2,1)} %all-gather.11.cloned.1.call-done, bf16[512,1024]{1,0:T(8,128)(2,1)S(1)} %copy-done), kind=kOutput, calls=%fused_computation.130 | convolution fusion | flops 2225077760 | bytes 15731712 | tf_op jit(solution)/shard_map/td,fd->tf/dot_general | solution.py:158
  258.6 4.3 convolution_convert_fusion
  263.0 4.6 multiply_convert_fusion.1
  268.9 4.3 convolution_convert_fusion.1
  273.5 36.5 %reduce-scatter.9.cloned.1.call-done = bf16[256,1024]{1,0:T(8,128)(2,1)} async-done(((bf16[2048,1024]{1,0:T(8,128)(2,1)}), bf16[256,1024]{1,0:T(8,128)(2,1)}) %reduce-scatter.9.cloned.1.call-update) | async-done | bytes 524304 | tf_op jit(solution)/shard_map/reduce_scatter | solution.py:165
  311.5 49.0 %reduce-scatter.7.cloned.1.call-done = bf16[256,1024]{1,0:T(8,128)(2,1)} async-done(((bf16[2048,1024]{1,0:T(8,128)(2,1)}), bf16[256,1024]{1,0:T(8,128)(2,1)}) %reduce-scatter.7.cloned.1.call-update) | async-done | bytes 524304 | tf_op jit(solution)/shard_map/reduce_scatter | solution.py:146
  360.5 2.5 fusion.79
  365.2 6.4 convolution_convert_fusion.5
  371.6 3.3 convolution_convert_fusion.4
  374.9 37.5 %all-gather.13.cloned.1.call-done = bf16[2048,1024]{1,0:T(8,128)(2,1)} async-done(((bf16[256,1024]{1,0:T(8,128)(2,1)}), bf16[2048,1024]{1,0:T(8,128)(2,1)}) %all-gather.13.cloned.1.call-update) | async-done | bytes 4194320 | tf_op jit(solution)/shard_map/all_gather | solution.py:176
  412.5 4.2 convolution_convert_fusion.3
  416.7 3.2 reshape.180
  419.9 3.5 copy.46
  423.4 3.8 convolution_convert_fusion.6
  427.5 49.0 %while.48 = (s32[]{:T(128)}, f32[2048,2,64]{0,2,1:T(8,128)S(1)}, f32[2048,2,64]{0,2,1:T(8,128)S(1)}, bf16[4,512,2,64]{1,3,2,0:T(8,128)(2,1)}, bf16[4,512,2,64]{1...) while((s32[]{:T(128)}, f32[2048,2,64]{0,2,1:T(8,128)S(1)}, ...), condition=%wide.region_15.16_spmd.clone, body=%wide.region_13.15_spmd.clone.sunk | while | flops 1368718336 | bytes 77885704 | solution.py:93
  427.5 2.2 fusion.144
  429.8 1.9 fusion.146
  431.7 2.4 multiply_reduce_fusion.6
  434.2 2.1 multiply_convert_fusion.3
  437.7 2.0 fusion.145
  439.8 2.3 fusion.144
  442.1 1.9 fusion.146
  444.0 2.4 multiply_reduce_fusion.6
  446.5 2.1 multiply_convert_fusion.3
  449.9 2.0 fusion.145
  452.0 2.3 fusion.144
  454.3 1.9 fusion.146
  456.2 2.4 multiply_reduce_fusion.6
  458.7 2.1 multiply_convert_fusion.3
  462.2 2.0 fusion.145
  464.3 2.3 fusion.144
  466.6 1.9 fusion.146
  468.5 2.4 multiply_reduce_fusion.6
  471.0 2.1 multiply_convert_fusion.3
  474.4 2.0 fusion.145
  476.5 3.6 copy.58
  480.1 3.1 reshape.181
  483.9 5.4 fusion.55
  489.3 2.3 copy.52
  491.7 4.3 bitcast_convert_fusion
  496.4 9.3 %all-reduce.1 = (bf16[2,128]{1,0:T(2,128)(2,1)S(1)}, bf16[512]{0:T(512)(128)(2,1)S(1)}) all-reduce(bf16[2,128]{1,0:T(2,128)(2,1)S(1)} %pad_maximum_fusion.4, bf16[512]{0:T(512)(128)(2,1)S(1)} %get-tuple-element.273), channel_id=1, replica_groups=mesh['dp'=4,'tensor'=8] {'dp'}, use_global_device_ids=true, to_apply=%region_21.22 | all-reduce | flops 768 | bytes 3072 | tf_op jit(solution)/shard_map/psum | solution.py:213
  506.8 1.9 convert_element_type.142
  508.7 2.8 convert_element_type.145
  513.1 34.0 %all-gather.15.cloned.1.call-done = bf16[12,1024,128]{2,1,0:T(8,128)(2,1)} async-done(((bf16[3,1024,128]{2,1,0:T(8,128)(2,1)}), bf16[12,1024,128]{2,1,0:T(8,128)(2,1)}) %all-gather.15.cloned.1.call-update) | async-done | bytes 3145744 | tf_op jit(solution)/shard_map/all_gather | solution.py:212
  547.1 3.6 reduce_sum.217
  550.7 2.4 copy.60
  553.1 2.5 copy.54
  555.6 40.5 %reduce-scatter.11.cloned.1.call-done = bf16[256,1024]{1,0:T(8,128)(2,1)} async-done(((bf16[2048,1024]{1,0:T(8,128)(2,1)}), bf16[256,1024]{1,0:T(8,128)(2,1)}) %reduce-scatter.11.cloned.1.call-update) | async-done | bytes 524304 | tf_op jit(solution)/shard_map/reduce_scatter | solution.py:201
  599.2 2.4 convert_reduce_fusion.3
  601.6 43.9 %all-reduce = (f32[1024]{0:T(1024)}, f32[2,1024]{1,0:T(2,128)}, f32[2,1024]{1,0:T(2,128)}, f32[1024]{0:T(1024)}) all-reduce(f32[1024]{0:T(1024)S(1)} %get-tuple-element.271, f32[2,1024]{1,0:T(2,128)S(1)} %get-tuple-element.296, f32[2,1024]{1,0:T(2,128)S(1)} %get-tuple-element.297, ...), channel_id=1, replica_groups=mesh['dp'=4,'tensor'=8] {'dp','tensor'}, use_global_device_ids=true, to_apply=%region_24.25 | all-reduce | flops 6144 | bytes 49152 | tf_op jit(solution)/shard_map/psum | solution.py:223
  (181 shorter events, 45.2 us)
Async XLA Ops:
  7.2 235.0 %copy-start = (bf16[512,1024]{1,0:T(8,128)(2,1)S(1)}, bf16[512,1024]{1,0:T(8,128)(2,1)}, u32[]{:S(2)}) copy-start(bf16[512,1024]{1,0:T(8,128)(2,1)} %param.25) | copy-start | bytes 3145732
  7.2 8.5 %copy-start.32 = (f32[2,128]{1,0:T(2,128)S(1)}, f32[2,128]{1,0:T(2,128)}, u32[]{:S(2)}) copy-start(f32[2,128]{1,0:T(2,128)} %param.18) | copy-start | bytes 3076
  7.2 53.8 %all-gather.7.cloned.1.call-start = ((), (), s32[]{:S(2)}) async-start(), calls=%async_computation.4 | async-start | bytes 4718592 | tf_op jit(solution)/shard_map/all_gather | solution.py:122
  8.5 5.7 copy-start.24
  9.9 0.6 copy-start.28
  10.4 3.7 copy-start.26
  11.2 3.0 copy-start.22
  14.2 128.7 %reduce-scatter.5.cloned.1.call-start = ((), (), s32[]{:S(2)}) async-start(), calls=%async_computation.5 | async-start | bytes 4718592 | tf_op jit(solution)/shard_map/reduce_scatter | solution.py:133
  65.9 26.6 %copy-start.20 = (bf16[128,1024]{1,0:T(8,128)(2,1)S(1)}, bf16[128,1024]{1,0:T(8,128)(2,1)}, u32[]{:S(2)}) copy-start(bf16[128,1024]{1,0:T(8,128)(2,1)} %param.19) | copy-start | bytes 786436
  89.7 2.0 copy-start.3
  89.7 6.1 copy-start.6
  91.7 0.8 copy-start.9
  95.8 47.0 %copy-start.2 = (bf16[256,1024]{1,0:T(8,128)(2,1)S(1)}, bf16[256,1024]{1,0:T(8,128)(2,1)}, u32[]{:S(2)}) copy-start(bf16[256,1024]{1,0:T(8,128)(2,1)} %param.16) | copy-start | bytes 1572868
  95.8 47.0 %copy-start.21 = (f32[1024]{0:T(1024)S(1)}, f32[1024]{0:T(1024)}, u32[]{:S(2)}) copy-start(f32[1024]{0:T(1024)} %param.20) | copy-start | bytes 12292
  95.8 99.2 %all-gather.9.cloned.1.call-start = ((), (), s32[]{:S(2)}) async-start(), calls=%async_computation.6 | async-start | bytes 4718592 | tf_op jit(solution)/shard_map/all_gather | solution.py:141
  147.7 94.5 %all-gather.11.cloned.1.call-start = ((), (), s32[]{:S(2)}) async-start(), calls=%async_computation.8 | async-start | bytes 4718592 | tf_op jit(solution)/shard_map/all_gather | solution.py:154
  148.2 93.9 %copy-start.31 = (f32[512]{0:T(512)S(1)}, f32[512]{0:T(512)}, u32[]{:S(2)}) copy-start(f32[512]{0:T(512)} %param.24) | copy-start | bytes 6148
  148.3 161.7 %reduce-scatter.9.cloned.1.call-start = ((), (), s32[]{:S(2)}) async-start(), calls=%async_computation.9 | async-start | bytes 4718592 | tf_op jit(solution)/shard_map/reduce_scatter | solution.py:165
  242.2 16.4 %copy-start.34 = (bf16[1024,512]{1,0:T(8,128)(2,1)S(1)}, bf16[1024,512]{1,0:T(8,128)(2,1)}, u32[]{:S(2)}) copy-start(bf16[1024,512]{1,0:T(8,128)(2,1)} %param.23) | copy-start | bytes 3145732
  257.3 1.3 copy-start.35
  262.9 97.6 %reduce-scatter.7.cloned.1.call-start = ((), (), s32[]{:S(2)}) async-start(), calls=%async_computation.7 | async-start | bytes 4718592 | tf_op jit(solution)/shard_map/reduce_scatter | solution.py:146
  267.6 1.3 copy-start.14
  273.2 36.8 %copy-start.5 = (bf16[256,1024]{1,0:T(8,128)(2,1)S(1)}, bf16[256,1024]{1,0:T(8,128)(2,1)}, u32[]{:S(2)}) copy-start(bf16[256,1024]{1,0:T(8,128)(2,1)} %reduce-scatter.5.cloned.1.call-done) | copy-start | bytes 1572868
  273.2 87.3 %copy-start.30 = (f32[1024]{0:T(1024)S(1)}, f32[1024]{0:T(1024)}, u32[]{:S(2)}) copy-start(f32[1024]{0:T(1024)} %param.26) | copy-start | bytes 12292
  273.2 90.9 %copy-start.11 = (bf16[256,1024]{1,0:T(8,128)(2,1)S(1)}, bf16[256,1024]{1,0:T(8,128)(2,1)}, u32[]{:S(2)}) copy-start(bf16[256,1024]{1,0:T(8,128)(2,1)} %param.27) | copy-start | bytes 1572868
  273.2 139.2 %all-gather.13.cloned.1.call-start = ((), (), s32[]{:S(2)}) async-start(), calls=%async_computation.10 | async-start | bytes 4718592 | tf_op jit(solution)/shard_map/all_gather | solution.py:176
  363.1 1.0 copy-start.7
  365.1 141.7 %all-reduce.5.cloned.1.call-start = ((), (), s32[]{:S(2)}) async-start(), calls=%async_computation.13 | async-start | bytes 4718592 | tf_op jit(solution)/shard_map/psum | solution.py:214
  365.2 6.4 copy-start.15
  365.2 6.4 copy-start.33
  427.2 119.9 %all-gather.15.cloned.1.call-start = ((), (), s32[]{:S(2)}) async-start(), calls=%async_computation.12 | async-start | bytes 3932160 | tf_op jit(solution)/shard_map/all_gather | solution.py:212
  427.5 2.3 copy-start.10
  429.8 1.9 copy-start.4
  434.2 2.1 copy-start.18
  437.7 2.0 copy-start.19
  439.8 2.3 copy-start.10
  442.0 1.9 copy-start.4
  446.4 2.1 copy-start.18
  449.9 2.1 copy-start.19
  452.0 2.3 copy-start.10
  454.3 1.9 copy-start.4
  458.7 2.1 copy-start.18
  462.2 2.1 copy-start.19
  464.3 2.3 copy-start.10
  466.6 1.9 copy-start.4
  471.0 2.1 copy-start.18
  474.4 2.1 copy-start.19
  483.9 7.8 %copy-start.13 = (bf16[2048,1,128]{2,0,1:T(8,128)(2,1)S(1)}, bf16[2048,1,128]{2,0,1:T(8,128)(2,1)}, u32[]{:S(2)}) copy-start(bf16[2048,1,128]{2,0,1:T(8,128)(2,1)} %reshape.181) | copy-start | bytes 1572868
  483.9 7.8 %copy-start.17 = (bf16[3,1024,128]{2,1,0:T(8,128)(2,1)S(1)}, bf16[3,1024,128]{2,1,0:T(8,128)(2,1)}, u32[]{:S(2)}) copy-start(bf16[3,1024,128]{2,1,0:T(8,128)(2,1)} %param.17) | copy-start | bytes 2359300
  491.6 104.4 %reduce-scatter.11.cloned.1.call-start = ((), (), s32[]{:S(2)}) async-start(), calls=%async_computation.11 | async-start | bytes 4718592 | tf_op jit(solution)/shard_map/reduce_scatter | solution.py:201
  506.8 4.7 copy-start.16
  513.1 83.0 %copy-start.23 = (f32[1,1024]{1,0:T(1,128)S(1)}, f32[1,1024]{1,0:T(1,128)}, u32[]{:S(2)}) copy-start(f32[1,1024]{1,0:T(1,128)} %copy-done.22) | copy-start | bytes 12292
  513.1 83.0 %copy-start.25 = (f32[256]{0:T(256)S(1)}, f32[256]{0:T(256)}, u32[]{:S(2)}) copy-start(f32[256]{0:T(256)} %copy-done.24) | copy-start | bytes 3076
  547.1 50.4 %copy-start.29 = (f32[256]{0:T(256)S(1)}, f32[256]{0:T(256)}, u32[]{:S(2)}) copy-start(f32[256]{0:T(256)} %copy-done.28) | copy-start | bytes 3076
  547.1 50.4 %copy-start.27 = (f32[256]{0:T(256)S(1)}, f32[256]{0:T(256)}, u32[]{:S(2)}) copy-start(f32[256]{0:T(256)} %copy-done.26) | copy-start | bytes 3076
  547.1 52.1 %copy-start.8 = (f32[256,1024]{1,0:T(8,128)S(1)}, f32[256,1024]{1,0:T(8,128)}, u32[]{:S(2)}) copy-start(f32[256,1024]{1,0:T(8,128)} %copy-done.7) | copy-start | bytes 3145732
  547.1 52.1 %copy-start.12 = (bf16[256,1024]{1,0:T(8,128)(2,1)S(1)}, bf16[256,1024]{1,0:T(8,128)(2,1)}, u32[]{:S(2)}) copy-start(bf16[256,1024]{1,0:T(8,128)(2,1)} %param.27) | copy-start | bytes 1572868
  550.7 94.9 %copy-start.1 = (bf16[512,1024]{1,0:T(8,128)(2,1)S(1)}, bf16[512,1024]{1,0:T(8,128)(2,1)}, u32[]{:S(2)}) copy-start(bf16[512,1024]{1,0:T(8,128)(2,1)} %param.25) | copy-start | bytes 3145732
Sparse Core Ops, SparseCore 0:
  14.3 46.7 all-gather.6
  95.9 46.8 reduce-scatter.4
  147.8 47.1 all-gather.8
  196.5 45.6 all-gather.10
  263.1 46.8 reduce-scatter.8
  312.1 48.3 reduce-scatter.6
  365.2 47.1 all-gather.12
  427.3 73.8 all-reduce.4
  503.0 43.9 all-gather.14
  549.2 46.7 reduce-scatter.10
